TPU v7x, 128 devices: a whole 4x4x4 slice. The times are simulated.
128 devices in a mesh: row: 8 (over x, z_lo), col: 16 (over z_hi, y, core).
Axes of the slice: x: 4, y: 4, z: 4 (z_hi: 2, z_lo: 2; z = z_hi * 2 + z_lo), core: 2. Of those that a mesh axis runs over, the one named last changes fastest.
Arguments:
- a_cols: bfloat16 [16384, 8192], P('row', 'col'), may hold values from -6 to 6
- owners: int32 [1024], replicated, may hold values from 0 to 15
- column_slot: int32 [1024], replicated, may hold values from 0 to 511
- update_flag: int32 [1024], replicated, may hold values from 0 to 1
- rescale: float32 [1024], replicated, may hold values from 0.5 to 2
- inverses: bfloat16 [2, 512, 512], replicated, may hold values from -0.0078125 to 0.0078125
- trailing: float32 [16384, 16384], P('row', 'col'), may hold values from -0.15625 to 0.15625
Outputs:
- updated_slab: float32 [16384, 16384], P('row', 'col')
- panels: bfloat16 [16384, 1024], P('row')
All inputs are finite; a program needn't handle non-finite values.
Results may differ from a plain program's by a relative error of at most 0.013.
The roundings to bfloat16 on the way count: a program that leaves them out, or rounds other values in their place, can miss the bound.
Values may be sent and summed in bfloat16 or wider, within the bound.
No kernel may reach another device: no remote copies, remote signals or barrier semaphores. Data moves between devices by JAX's collectives and lax.ppermute only.
A program may use at most 128 MiB of HBM per device.

v0:
```python
import jax
import jax.numpy as jnp
from jax import lax
from jax.experimental import pallas as pl
from jax.experimental.pallas import tpu as pltpu
from jax.sharding import PartitionSpec as P


BF = jnp.bfloat16
F32 = jnp.float32


def move(value, route):
    pairs = []
    for x in range(4):
        for zl in range(2):
            for zh in range(2):
                for y in range(4):
                    for k in range(2):
                        x2, zl2, zh2, y2, k2 = route(x, zl, zh, y, k)
                        source = (x * 2 + zl) * 16 + zh * 8 + y * 2 + k
                        target = (x2 % 4 * 2 + zl2) * 16 + zh2 * 8 + y2 % 4 * 2 + k2
                        pairs.append((source, target))
    return lax.ppermute(value, ("row", "col"), pairs)


def other_core(x, zl, zh, y, k):
    return x, zl, zh, y, 1 - k


def other_zh(x, zl, zh, y, k):
    return x, zl, 1 - zh, y, k


def other_zl(x, zl, zh, y, k):
    return x, 1 - zl, zh, y, k


def along_y(step):
    return lambda x, zl, zh, y, k: (x, zl, zh, y + step, k)


def along_x(step):
    return lambda x, zl, zh, y, k: (x + step, zl, zh, y, k)


def flip_x(bit):
    return lambda x, zl, zh, y, k: (x ^ bit, zl, zh, y, k)


def to_strip(x, zl, zh, y, k):
    zh2 = x // 2
    return x + y, zh ^ zl ^ zh2, zh2, (x % 2) * 2 + zl, k


def rows(value, start, count):
    return lax.dynamic_slice_in_dim(value, start, count, 0)


def put(buffer, piece, start):
    return lax.dynamic_update_slice_in_dim(buffer, piece, start, 0)


def mm(a, b):
    return jnp.dot(a, b, preferred_element_type=F32)


def to_chip(step, dz):
    return lambda x, zl, zh, y, k: (x, zl, zh ^ dz, y + step, k)


def finish_kernel(spot, *refs):
    pieces = refs[:12]
    gram_ref, inverse_ref, sign_ref, trailing_ref, out_ref, panel_ref, strip_ref, now_ref = refs[12:]
    t = pl.program_id(0)
    for i in range(12):

        @pl.when(t == i)
        def _():
            now_ref[...] = pieces[i][...]

    sign = sign_ref[...]
    first = mm(now_ref[:, :512], inverse_ref[0]).astype(BF)
    first_signed = first * sign[:, :512]
    coupled = (now_ref[:, 512:].astype(F32) - mm(first_signed, gram_ref[...])).astype(BF)
    second = mm(coupled, inverse_ref[1]).astype(BF)

    @pl.when(t < 4)
    def _():
        at = pl.ds(pl.multiple_of(spot[t] * 256, 256), 256)
        strip_ref[at, :512] = first
        strip_ref[at, 512:] = second

    @pl.when(t >= 4)
    def _():
        panel_ref[:, :512] = first
        panel_ref[:, 512:] = second
        across = (((1,), (1,)), ((), ()))
        update = lax.dot_general(
            first_signed, strip_ref[:, :512], across, preferred_element_type=F32
        )
        update += lax.dot_general(
            second * sign[:, 512:], strip_ref[:, 512:], across, preferred_element_type=F32
        )
        out_ref[...] = trailing_ref[...] + update


def finish(spot, strips, block, gram_low, inverses, sign, trailing):
    def whole(value):
        zeros = (0,) * value.ndim
        return pl.BlockSpec(
            value.shape, lambda t, spot: zeros, pipeline_mode=pl.Buffered(1)
        )

    def tile(width):
        return pl.BlockSpec((256, width), lambda t, spot: (spot[jnp.maximum(t, 4)], 0))

    fixed = [*strips, *block, gram_low, inverses, sign]
    return pl.pallas_call(
        finish_kernel,
        grid_spec=pltpu.PrefetchScalarGridSpec(
            num_scalar_prefetch=1,
            grid=(12,),
            in_specs=[whole(value) for value in fixed] + [tile(1024)],
            out_specs=[tile(1024), tile(1024)],
            scratch_shapes=[pltpu.VMEM((1024, 1024), BF), pltpu.VMEM((256, 1024), BF)],
        ),
        out_shape=(
            jax.ShapeDtypeStruct((2048, 1024), F32),
            jax.ShapeDtypeStruct((2048, 1024), BF),
        ),
        compiler_params=pltpu.CompilerParams(vmem_limit_bytes=40 * 2**20),
        cost_estimate=pl.CostEstimate(
            flops=9_000_000_000, bytes_accessed=26 * 2**20, transcendentals=0
        ),
    )(spot, *fixed, trailing)


def body(a_cols, owners, column_slot, update_flag, rescale, inverses, trailing):
    col = lax.axis_index("col")
    row = lax.axis_index("row")
    k, y, zh = col % 2, (col // 2) % 4, col // 8
    x, zl = row // 2, row % 2
    signed = (2 * update_flag - 1).astype(BF)

    keep = rows(a_cols, k * 1024, 1024)
    got = move(rows(a_cols, (1 - k) * 1024, 1024), other_core)
    both = jnp.concatenate([keep, got], axis=1)
    ok, oy, oz = owners % 2, (owners // 2) % 4, owners // 8
    place = (ok ^ k) * 512 + column_slot
    slots = lax.broadcasted_iota(jnp.int32, (1024, 1024), 0)
    picked = None
    for dz in (0, 1):
        for step in (0, 1, 2, 3):
            piece = rows(both, (y + step) % 4 * 256 + (zh ^ dz) * 128, 128)
            if dz or step:
                piece = move(piece, to_chip(step, dz))
            held = (oz == (zh ^ dz)) & ((y - oy) % 4 == step)
            select = (slots == jnp.where(held, place, -1)[None, :]).astype(BF)
            term = mm(piece, select)
            picked = term if picked is None else picked + term
    cols = (picked * rescale[None, :]).astype(BF)

    pair = put(jnp.zeros((256, 1024), BF), cols, zh * 128)
    pair = put(pair, move(cols, other_zh), (1 - zh) * 128)

    first = zh * 2 + y // 2
    part = zl ^ (y % 2) ^ zh
    piece = move(cols, to_strip)
    strip = put(jnp.zeros((256, 1024), BF), piece, part * 128)
    strip = put(strip, move(piece, other_zl), (1 - part) * 128)
    strips = [strip] + [move(strip, along_x(step)) for step in (1, 2, 3)]

    near = [pair] + [move(pair, along_y(step)) for step in (1, 2, 3)]
    far = [move(value, other_core) for value in near]

    fp = mm(pair[:, :512], inverses[0]).astype(BF)
    right = lax.dynamic_slice_in_dim(pair, 512 + zh * 256, 256, 1)
    gram = lax.dot_general(fp, right, (((0,), (0,)), ((), ())), preferred_element_type=F32)
    gram = rows(gram, k * 256, 256) + move(rows(gram, (1 - k) * 256, 256), other_core)
    total = rows(gram, y * 64, 64)
    for step in (1, 2, 3):
        total = total + move(rows(gram, ((y + step) % 4) * 64, 64), along_y(step))
    total = total + move(total, other_zl)
    total = total + move(total, flip_x(1))
    total = total + move(total, flip_x(2))
    low = total.astype(BF)
    low2 = jnp.zeros((64, 512), BF)
    low2 = lax.dynamic_update_slice_in_dim(low2, low, zh * 256, 1)
    low2 = lax.dynamic_update_slice_in_dim(low2, move(low, other_zh), (1 - zh) * 256, 1)
    low3 = put(jnp.zeros((256, 512), BF), low2, y * 64)
    for step in (1, 2, 3):
        low3 = put(low3, move(low2, along_y(step)), ((y - step) % 4) * 64)
    low4 = put(jnp.zeros((512, 512), BF), low3, k * 256)
    gram_low = put(low4, move(low3, other_core), (1 - k) * 256)

    tile = lax.iota(jnp.int32, 12)
    step = tile % 4
    spot = jnp.where(
        tile < 4,
        (x - step - first) % 4,
        jnp.where(tile < 8, k, 1 - k) * 4 + (y - step) % 4,
    )
    return finish(spot, strips, near + far, gram_low, inverses, signed[None, :], trailing)


def solution(mesh):
    placed = (P("row", "col"), P(), P(), P(), P(), P(), P("row", "col"))
    return jax.shard_map(
        body,
        mesh=mesh,
        in_specs=placed,
        out_specs=(P("row", "col"), P("row", None)),
        check_vma=False,
    )
```

profile of v0, /device:TPU:1, one launch (start us, length us, event | category | flops | bytes accessed | tf_op | source)
XLA Modules:
  0.0 151.3 jit_solution(5421256786937935096)
XLA Ops:
  0.7 1.7 %constant_dynamic-slice_fusion.4 = (bf16[1024,512]{1,0:T(8,128)(2,1)S(1)}, bf16[1024,512]{1,0:T(8,128)(2,1)S(1)}) fusion(bf16[2048,512]{1,0:T(8,128)(2,1)} %param.7, s32[]{:T(128)S(6)} %select_n.252, s32[]{:T(128)S(6)} %select_n.251), kind=kLoop, calls=%fused_computation.84 | loop fusion | bytes 4194312 | tf_op jit(solution)/shard_map/dynamic_slice | solution.py:57
  3.9 2.2 %collective-permute-done = bf16[1024,512]{1,0:T(8,128)(2,1)S(1)} collective-permute-done((bf16[1024,512]{1,0:T(8,128)(2,1)S(1)}, bf16[1024,512]{1,0:T(8,128)(2,1)S(1)}, u32[]{:S(2)}, u32[]{:S(2)}) %collective-permute-start) | collective-permute-done | bytes 1048608 | tf_op jit(solution)/shard_map/ppermute | solution.py:24
  6.1 6.2 %collective-permute-start.7 = (bf16[128,1024]{1,0:T(8,128)(2,1)S(1)}, bf16[128,1024]{1,0:T(8,128)(2,1)}, u32[]{:S(2)}, u32[]{:S(2)}) collective-permute-start(bf16[128,1024]{1,0:T(8,128)(2,1)S(1)} %fusion.30), channel_id=1, source_target_pairs={{0,14},{1,15},{2,8},{3,9},{4,10},{5,11},{6,12},{7,13},{8,6},{9,7},... | collective-permute-start | bytes 786440 | tf_op jit(solution)/shard_map/ppermute | solution.py:24
  16.1 5.9 %collective-permute-done.7 = bf16[128,1024]{1,0:T(8,128)(2,1)} collective-permute-done((bf16[128,1024]{1,0:T(8,128)(2,1)S(1)}, bf16[128,1024]{1,0:T(8,128)(2,1)}, u32[]{:S(2)}, u32[]{:S(2)}) %collective-permute-start.7) | collective-permute-done | bytes 262176 | tf_op jit(solution)/shard_map/ppermute | solution.py:24
  22.0 1.9 %fusion.7 = f32[128,1024]{1,0:T(8,128)S(1)} fusion(bf16[128,1024]{1,0:T(8,128)(2,1)} %collective-permute-done.7, s32[1024]{0:T(1024)S(1)} %get-tuple-element.34), kind=kOutput, calls=%fused_computation.15 | convolution fusion | flops 269484032 | bytes 790528 | tf_op jit(solution)/shard_map/dot_general | solution.py:65
  23.9 2.4 %collective-permute-start.6 = (bf16[128,1024]{1,0:T(8,128)(2,1)S(1)}, bf16[128,1024]{1,0:T(8,128)(2,1)S(1)}, u32[]{:S(2)}, u32[]{:S(2)}) collective-permute-start(bf16[128,1024]{1,0:T(8,128)(2,1)S(1)} %get-tuple-element.22), channel_id=1, source_target_pairs={{0,12},{1,13},{2,14},{3,15},{4,8},{5,9},{6,10},{7,11},{8,4},{9,5},... | collective-permute-start | bytes 786440 | tf_op jit(solution)/shard_map/ppermute | solution.py:24
  26.3 1.9 %fusion.1 = f32[128,1024]{1,0:T(8,128)S(1)} fusion(bf16[128,1024]{1,0:T(8,128)(2,1)} %collective-permute-done.1, s32[1024]{0:T(1024)S(1)} %get-tuple-element.9), kind=kOutput, calls=%fused_computation.9 | convolution fusion | flops 269484032 | bytes 790528 | tf_op jit(solution)/shard_map/dot_general | solution.py:65
  31.1 6.0 %collective-permute-done.5 = bf16[128,1024]{1,0:T(8,128)(2,1)S(1)} collective-permute-done((bf16[128,1024]{1,0:T(8,128)(2,1)S(1)}, bf16[128,1024]{1,0:T(8,128)(2,1)S(1)}, u32[]{:S(2)}, u32[]{:S(2)}) %collective-permute-start.5) | collective-permute-done | bytes 262176 | tf_op jit(solution)/shard_map/ppermute | solution.py:24
  40.2 3.5 %collective-permute-start.13 = (bf16[128,1024]{1,0:T(8,128)(2,1)S(1)}, bf16[128,1024]{1,0:T(8,128)(2,1)S(1)}, u32[]{:S(2)}, u32[]{:S(2)}) collective-permute-start(bf16[128,1024]{1,0:T(8,128)(2,1)S(1)} %get-tuple-element.38), channel_id=1, source_target_pairs={{0,8},{1,9},{2,10},{3,11},{4,12},{5,13},{6,14},{7,15},{8,0},{9,1},... | collective-permute-start | bytes 786440 | tf_op jit(solution)/shard_map/ppermute | solution.py:24
  43.6 3.8 %collective-permute-done.13 = bf16[128,1024]{1,0:T(8,128)(2,1)S(1)} collective-permute-done((bf16[128,1024]{1,0:T(8,128)(2,1)S(1)}, bf16[128,1024]{1,0:T(8,128)(2,1)S(1)}, u32[]{:S(2)}, u32[]{:S(2)}) %collective-permute-start.13) | collective-permute-done | bytes 262176 | tf_op jit(solution)/shard_map/ppermute | solution.py:24
  48.1 5.5 %collective-permute-start.21 = (f32[256,256]{1,0:T(8,128)S(1)}, f32[256,256]{1,0:T(8,128)S(1)}, u32[]{:S(2)}, u32[]{:S(2)}) collective-permute-start(f32[256,256]{1,0:T(8,128)S(1)} %constant_dynamic-slice_fusion.3), channel_id=1, source_target_pairs={{0,1},{1,0},{2,3},{3,2},{4,5},{5,4},{6,7},{7,6},{8,9},{9,8},{10,11... | collective-permute-start | bytes 786440 | tf_op jit(solution)/shard_map/ppermute | solution.py:24
  54.9 2.7 %collective-permute-start.24 = (f32[64,256]{1,0:T(8,128)S(1)}, f32[64,256]{1,0:T(8,128)S(1)}, u32[]{:S(2)}, u32[]{:S(2)}) collective-permute-start(f32[64,256]{1,0:T(8,128)S(1)} %get-tuple-element.26), channel_id=1, source_target_pairs={{0,6},{1,7},{2,0},{3,1},{4,2},{5,3},{6,4},{7,5},{8,14},{9,15},{10,... | collective-permute-start | bytes 196616 | tf_op jit(solution)/shard_map/ppermute | solution.py:24
  60.2 1.9 %collective-permute-done.23 = f32[64,256]{1,0:T(8,128)S(1)} collective-permute-done((f32[64,256]{1,0:T(8,128)S(1)}, f32[64,256]{1,0:T(8,128)S(1)}, u32[]{:S(2)}, u32[]{:S(2)}) %collective-permute-start.23) | collective-permute-done | bytes 65568 | tf_op jit(solution)/shard_map/ppermute | solution.py:24
  63.5 1.8 %collective-permute-done.25 = f32[64,256]{1,0:T(8,128)S(1)} collective-permute-done((f32[64,256]{1,0:T(8,128)S(1)}, f32[64,256]{1,0:T(8,128)S(1)}, u32[]{:S(2)}, u32[]{:S(2)}) %collective-permute-start.25) | collective-permute-done | bytes 65568 | tf_op jit(solution)/shard_map/ppermute | solution.py:24
  67.0 3.2 %collective-permute-start.17 = (bf16[256,1024]{1,0:T(8,128)(2,1)S(1)}, bf16[256,1024]{1,0:T(8,128)(2,1)S(1)}, u32[]{:S(2)}, u32[]{:S(2)}) collective-permute-start(bf16[256,1024]{1,0:T(8,128)(2,1)S(1)} %constant_dynamic-update-slice_fusion.8.refs_4_), channel_id=1, source_target_pairs={{0,1},{1,0},{2,3},{3,2},{4,5},{5,4},{6,7},{7,6},{8,9},{9,8},{10,11... | collective-permute-start | bytes 1572872 | tf_op jit(solution)/shard_map/ppermute | solution.py:24
  71.9 4.2 %collective-permute-start.27 = (f32[64,256]{1,0:T(8,128)S(1)}, f32[64,256]{1,0:T(8,128)S(1)}, u32[]{:S(2)}, u32[]{:S(2)}) collective-permute-start(f32[64,256]{1,0:T(8,128)S(1)} %add.331), channel_id=1, source_target_pairs={{0,64},{1,65},{2,66},{3,67},{4,68},{5,69},{6,70},{7,71},{8,72},{9,... | collective-permute-start | bytes 196616 | tf_op jit(solution)/shard_map/ppermute | solution.py:24
  76.2 1.8 %collective-permute-done.27 = f32[64,256]{1,0:T(8,128)S(1)} collective-permute-done((f32[64,256]{1,0:T(8,128)S(1)}, f32[64,256]{1,0:T(8,128)S(1)}, u32[]{:S(2)}, u32[]{:S(2)}) %collective-permute-start.27) | collective-permute-done | bytes 65568 | tf_op jit(solution)/shard_map/ppermute | solution.py:24
  78.0 4.0 %collective-permute-start.28 = (bf16[64,256]{1,0:T(8,128)(2,1)S(1)}, bf16[64,256]{1,0:T(8,128)(2,1)S(1)}, u32[]{:S(2)}, u32[]{:S(2)}) collective-permute-start(bf16[64,256]{1,0:T(8,128)(2,1)S(1)} %get-tuple-element.3), channel_id=1, source_target_pairs={{0,8},{1,9},{2,10},{3,11},{4,12},{5,13},{6,14},{7,15},{8,0},{9,1},... | collective-permute-start | bytes 98312 | tf_op jit(solution)/shard_map/ppermute | solution.py:24
  87.0 1.8 %collective-permute-start.15 = (bf16[256,1024]{1,0:T(8,128)(2,1)S(1)}, bf16[256,1024]{1,0:T(8,128)(2,1)}, u32[]{:S(2)}, u32[]{:S(2)}) collective-permute-start(bf16[256,1024]{1,0:T(8,128)(2,1)S(1)} %constant_dynamic-update-slice_fusion.8.refs_4_), channel_id=1, source_target_pairs={{0,4},{1,5},{2,6},{3,7},{4,0},{5,1},{6,2},{7,3},{8,12},{9,13},{10,... | collective-permute-start | bytes 1572872 | tf_op jit(solution)/shard_map/ppermute | solution.py:24
  91.1 11.9 %collective-permute-start.32 = (bf16[256,512]{1,0:T(8,128)(2,1)S(1)}, bf16[256,512]{1,0:T(8,128)(2,1)}, u32[]{:S(2)}, u32[]{:S(2)}) collective-permute-start(bf16[256,512]{1,0:T(8,128)(2,1)S(1)} %constant_dynamic-update-slice_fusion.2), channel_id=1, source_target_pairs={{0,1},{1,0},{2,3},{3,2},{4,5},{5,4},{6,7},{7,6},{8,9},{9,8},{10,11... | collective-permute-start | bytes 786440 | tf_op jit(solution)/shard_map/ppermute | solution.py:24
  103.1 1.7 %collective-permute-start.11 = (bf16[256,1024]{1,0:T(8,128)(2,1)S(1)}, bf16[256,1024]{1,0:T(8,128)(2,1)}, u32[]{:S(2)}, u32[]{:S(2)}) collective-permute-start(bf16[256,1024]{1,0:T(8,128)(2,1)S(1)} %constant_dynamic-update-slice_fusion.10.refs_0_), channel_id=1, source_target_pairs={{0,64},{1,65},{2,66},{3,67},{4,68},{5,69},{6,70},{7,71},{8,72},{9,... | collective-permute-start | bytes 1572872 | tf_op jit(solution)/shard_map/ppermute | solution.py:24
  105.9 8.6 %collective-permute-done.14.refs_5_ = bf16[256,1024]{1,0:T(8,128)(2,1)} collective-permute-done((bf16[256,1024]{1,0:T(8,128)(2,1)S(1)}, bf16[256,1024]{1,0:T(8,128)(2,1)}, u32[]{:S(2)}, u32[]{:S(2)}) %collective-permute-start.14) | collective-permute-done | bytes 524320 | tf_op jit(solution)/shard_map/ppermute | solution.py:24
  118.1 11.7 %collective-permute-done.10.refs_1_ = bf16[256,1024]{1,0:T(8,128)(2,1)} collective-permute-done((bf16[256,1024]{1,0:T(8,128)(2,1)S(1)}, bf16[256,1024]{1,0:T(8,128)(2,1)}, u32[]{:S(2)}, u32[]{:S(2)}) %collective-permute-start.10) | collective-permute-done | bytes 524320 | tf_op jit(solution)/shard_map/ppermute | solution.py:24
  129.8 21.5 %shard_map.86 = (f32[2048,1024]{1,0:T(8,128)}, bf16[2048,1024]{1,0:T(8,128)(2,1)}) custom-call(s32[12]{0:T(128)S(1)} %compare_select_fusion.5.spot, bf16[256,1024]{1,0:T(8,128)(2,1)S(1)} %constant_dynamic-update-slice_fusion.10.refs_0_, bf16[256,1024]{1,0:T(8,128)(2,1)} %collective-permute-done.10.refs_1_, ...), custom_call_target="tpu_custom_call" | custom-call | flops 8999999488 | bytes 27262976 | tf_op jit(solution)/shard_map/pallas_call | solution.py:119
  (99 shorter events, 32.6 us)
Async XLA Ops:
  6.1 15.9 %collective-permute-start.7 = (bf16[128,1024]{1,0:T(8,128)(2,1)S(1)}, bf16[128,1024]{1,0:T(8,128)(2,1)}, u32[]{:S(2)}, u32[]{:S(2)}) collective-permute-start(bf16[128,1024]{1,0:T(8,128)(2,1)S(1)} %fusion.30), channel_id=1, source_target_pairs={{0,14},{1,15},{2,8},{3,9},{4,10},{5,11},{6,12},{7,13},{8,6},{9,7},... | collective-permute-start | bytes 786440 | tf_op jit(solution)/shard_map/ppermute | solution.py:24
  13.3 10.5 %collective-permute-start.1 = (bf16[128,1024]{1,0:T(8,128)(2,1)}, bf16[128,1024]{1,0:T(8,128)(2,1)}, u32[]{:S(2)}, u32[]{:S(2)}) collective-permute-start(bf16[128,1024]{1,0:T(8,128)(2,1)} %get-tuple-element.17), channel_id=1, source_target_pairs={{0,2},{1,3},{2,4},{3,5},{4,6},{5,7},{6,0},{7,1},{8,10},{9,11},{10,... | collective-permute-start | bytes 786440 | tf_op jit(solution)/shard_map/ppermute | solution.py:24
  13.4 14.8 %collective-permute-start.2 = (bf16[128,1024]{1,0:T(8,128)(2,1)}, bf16[128,1024]{1,0:T(8,128)(2,1)S(1)}, u32[]{:S(2)}, u32[]{:S(2)}) collective-permute-start(bf16[128,1024]{1,0:T(8,128)(2,1)} %get-tuple-element.18), channel_id=1, source_target_pairs={{0,4},{1,5},{2,6},{3,7},{4,0},{5,1},{6,2},{7,3},{8,12},{9,13},{10,... | collective-permute-start | bytes 786440 | tf_op jit(solution)/shard_map/ppermute | solution.py:24
  15.0 14.2 %collective-permute-start.3 = (bf16[128,1024]{1,0:T(8,128)(2,1)S(1)}, bf16[128,1024]{1,0:T(8,128)(2,1)S(1)}, u32[]{:S(2)}, u32[]{:S(2)}) collective-permute-start(bf16[128,1024]{1,0:T(8,128)(2,1)S(1)} %get-tuple-element.19), channel_id=1, source_target_pairs={{0,6},{1,7},{2,0},{3,1},{4,2},{5,3},{6,4},{7,5},{8,14},{9,15},{10,... | collective-permute-start | bytes 786440 | tf_op jit(solution)/shard_map/ppermute | solution.py:24
  16.1 14.0 %collective-permute-start.4 = (bf16[128,1024]{1,0:T(8,128)(2,1)S(1)}, bf16[128,1024]{1,0:T(8,128)(2,1)S(1)}, u32[]{:S(2)}, u32[]{:S(2)}) collective-permute-start(bf16[128,1024]{1,0:T(8,128)(2,1)S(1)} %get-tuple-element.20), channel_id=1, source_target_pairs={{0,8},{1,9},{2,10},{3,11},{4,12},{5,13},{6,14},{7,15},{8,0},{9,1},... | collective-permute-start | bytes 786440 | tf_op jit(solution)/shard_map/ppermute | solution.py:24
  22.0 15.1 %collective-permute-start.5 = (bf16[128,1024]{1,0:T(8,128)(2,1)S(1)}, bf16[128,1024]{1,0:T(8,128)(2,1)S(1)}, u32[]{:S(2)}, u32[]{:S(2)}) collective-permute-start(bf16[128,1024]{1,0:T(8,128)(2,1)S(1)} %get-tuple-element.21), channel_id=1, source_target_pairs={{0,10},{1,11},{2,12},{3,13},{4,14},{5,15},{6,8},{7,9},{8,2},{9,3},... | collective-permute-start | bytes 786440 | tf_op jit(solution)/shard_map/ppermute | solution.py:24
  23.9 14.1 %collective-permute-start.6 = (bf16[128,1024]{1,0:T(8,128)(2,1)S(1)}, bf16[128,1024]{1,0:T(8,128)(2,1)S(1)}, u32[]{:S(2)}, u32[]{:S(2)}) collective-permute-start(bf16[128,1024]{1,0:T(8,128)(2,1)S(1)} %get-tuple-element.22), channel_id=1, source_target_pairs={{0,12},{1,13},{2,14},{3,15},{4,8},{5,9},{6,10},{7,11},{8,4},{9,5},... | collective-permute-start | bytes 786440 | tf_op jit(solution)/shard_map/ppermute | solution.py:24
  40.2 7.2 %collective-permute-start.13 = (bf16[128,1024]{1,0:T(8,128)(2,1)S(1)}, bf16[128,1024]{1,0:T(8,128)(2,1)S(1)}, u32[]{:S(2)}, u32[]{:S(2)}) collective-permute-start(bf16[128,1024]{1,0:T(8,128)(2,1)S(1)} %get-tuple-element.38), channel_id=1, source_target_pairs={{0,8},{1,9},{2,10},{3,11},{4,12},{5,13},{6,14},{7,15},{8,0},{9,1},... | collective-permute-start | bytes 786440 | tf_op jit(solution)/shard_map/ppermute | solution.py:24
  48.1 6.6 %collective-permute-start.21 = (f32[256,256]{1,0:T(8,128)S(1)}, f32[256,256]{1,0:T(8,128)S(1)}, u32[]{:S(2)}, u32[]{:S(2)}) collective-permute-start(f32[256,256]{1,0:T(8,128)S(1)} %constant_dynamic-slice_fusion.3), channel_id=1, source_target_pairs={{0,1},{1,0},{2,3},{3,2},{4,5},{5,4},{6,7},{7,6},{8,9},{9,8},{10,11... | collective-permute-start | bytes 786440 | tf_op jit(solution)/shard_map/ppermute | solution.py:24
  58.6 13.0 %collective-permute-start.8 = (bf16[128,1024]{1,0:T(8,128)(2,1)}, bf16[128,1024]{1,0:T(8,128)(2,1)S(1)}, u32[]{:S(2)}, u32[]{:S(2)}) collective-permute-start(bf16[128,1024]{1,0:T(8,128)(2,1)} %copy-done.3), channel_id=1, source_target_pairs={{0,0},{1,1},{2,32},{3,33},{4,64},{5,65},{6,96},{7,97},{8,16},{9,17... | collective-permute-start | bytes 786440 | tf_op jit(solution)/shard_map/ppermute | solution.py:24
  65.4 6.5 %collective-permute-start.26 = (f32[64,256]{1,0:T(8,128)S(1)}, f32[64,256]{1,0:T(8,128)S(1)}, u32[]{:S(2)}, u32[]{:S(2)}) collective-permute-start(f32[64,256]{1,0:T(8,128)S(1)} %add.330), channel_id=1, source_target_pairs={{0,32},{1,33},{2,34},{3,35},{4,36},{5,37},{6,38},{7,39},{8,40},{9,... | collective-permute-start | bytes 196616 | tf_op jit(solution)/shard_map/ppermute | solution.py:24
  67.0 24.2 %collective-permute-start.17 = (bf16[256,1024]{1,0:T(8,128)(2,1)S(1)}, bf16[256,1024]{1,0:T(8,128)(2,1)S(1)}, u32[]{:S(2)}, u32[]{:S(2)}) collective-permute-start(bf16[256,1024]{1,0:T(8,128)(2,1)S(1)} %constant_dynamic-update-slice_fusion.8.refs_4_), channel_id=1, source_target_pairs={{0,1},{1,0},{2,3},{3,2},{4,5},{5,4},{6,7},{7,6},{8,9},{9,8},{10,11... | collective-permute-start | bytes 1572872 | tf_op jit(solution)/shard_map/ppermute | solution.py:24
  70.2 32.9 %collective-permute-start.16 = (bf16[256,1024]{1,0:T(8,128)(2,1)S(1)}, bf16[256,1024]{1,0:T(8,128)(2,1)S(1)}, u32[]{:S(2)}, u32[]{:S(2)}) collective-permute-start(bf16[256,1024]{1,0:T(8,128)(2,1)S(1)} %constant_dynamic-update-slice_fusion.8.refs_4_), channel_id=1, source_target_pairs={{0,6},{1,7},{2,0},{3,1},{4,2},{5,3},{6,4},{7,5},{8,14},{9,15},{10,... | collective-permute-start | bytes 1572872 | tf_op jit(solution)/shard_map/ppermute | solution.py:24
  71.6 10.4 %collective-permute-start.9 = (bf16[128,1024]{1,0:T(8,128)(2,1)S(1)}, bf16[128,1024]{1,0:T(8,128)(2,1)S(1)}, u32[]{:S(2)}, u32[]{:S(2)}) collective-permute-start(bf16[128,1024]{1,0:T(8,128)(2,1)S(1)} %collective-permute-done.8), channel_id=1, source_target_pairs={{0,16},{1,17},{2,18},{3,19},{4,20},{5,21},{6,22},{7,23},{8,24},{9,... | collective-permute-start | bytes 786440 | tf_op jit(solution)/shard_map/ppermute | solution.py:24
  71.9 6.1 %collective-permute-start.27 = (f32[64,256]{1,0:T(8,128)S(1)}, f32[64,256]{1,0:T(8,128)S(1)}, u32[]{:S(2)}, u32[]{:S(2)}) collective-permute-start(f32[64,256]{1,0:T(8,128)S(1)} %add.331), channel_id=1, source_target_pairs={{0,64},{1,65},{2,66},{3,67},{4,68},{5,69},{6,70},{7,71},{8,72},{9,... | collective-permute-start | bytes 196616 | tf_op jit(solution)/shard_map/ppermute | solution.py:24
  87.0 17.7 %collective-permute-start.15 = (bf16[256,1024]{1,0:T(8,128)(2,1)S(1)}, bf16[256,1024]{1,0:T(8,128)(2,1)}, u32[]{:S(2)}, u32[]{:S(2)}) collective-permute-start(bf16[256,1024]{1,0:T(8,128)(2,1)S(1)} %constant_dynamic-update-slice_fusion.8.refs_4_), channel_id=1, source_target_pairs={{0,4},{1,5},{2,6},{3,7},{4,0},{5,1},{6,2},{7,3},{8,12},{9,13},{10,... | collective-permute-start | bytes 1572872 | tf_op jit(solution)/shard_map/ppermute | solution.py:24
  88.8 25.7 %collective-permute-start.14 = (bf16[256,1024]{1,0:T(8,128)(2,1)S(1)}, bf16[256,1024]{1,0:T(8,128)(2,1)}, u32[]{:S(2)}, u32[]{:S(2)}) collective-permute-start(bf16[256,1024]{1,0:T(8,128)(2,1)S(1)} %constant_dynamic-update-slice_fusion.8.refs_4_), channel_id=1, source_target_pairs={{0,2},{1,3},{2,4},{3,5},{4,6},{5,7},{6,0},{7,1},{8,10},{9,11},{10,... | collective-permute-start | bytes 1572872 | tf_op jit(solution)/shard_map/ppermute | solution.py:24
  89.8 25.9 %collective-permute-start.12 = (bf16[256,1024]{1,0:T(8,128)(2,1)S(1)}, bf16[256,1024]{1,0:T(8,128)(2,1)}, u32[]{:S(2)}, u32[]{:S(2)}) collective-permute-start(bf16[256,1024]{1,0:T(8,128)(2,1)S(1)} %constant_dynamic-update-slice_fusion.10.refs_0_), channel_id=1, source_target_pairs={{0,96},{1,97},{2,98},{3,99},{4,100},{5,101},{6,102},{7,103},{8,104... | collective-permute-start | bytes 1572872 | tf_op jit(solution)/shard_map/ppermute | solution.py:24
  91.1 24.5 %collective-permute-start.32 = (bf16[256,512]{1,0:T(8,128)(2,1)S(1)}, bf16[256,512]{1,0:T(8,128)(2,1)}, u32[]{:S(2)}, u32[]{:S(2)}) collective-permute-start(bf16[256,512]{1,0:T(8,128)(2,1)S(1)} %constant_dynamic-update-slice_fusion.2), channel_id=1, source_target_pairs={{0,1},{1,0},{2,3},{3,2},{4,5},{5,4},{6,7},{7,6},{8,9},{9,8},{10,11... | collective-permute-start | bytes 786440 | tf_op jit(solution)/shard_map/ppermute | solution.py:24
  103.1 15.0 %collective-permute-start.11 = (bf16[256,1024]{1,0:T(8,128)(2,1)S(1)}, bf16[256,1024]{1,0:T(8,128)(2,1)}, u32[]{:S(2)}, u32[]{:S(2)}) collective-permute-start(bf16[256,1024]{1,0:T(8,128)(2,1)S(1)} %constant_dynamic-update-slice_fusion.10.refs_0_), channel_id=1, source_target_pairs={{0,64},{1,65},{2,66},{3,67},{4,68},{5,69},{6,70},{7,71},{8,72},{9,... | collective-permute-start | bytes 1572872 | tf_op jit(solution)/shard_map/ppermute | solution.py:24
  104.8 25.0 %collective-permute-start.10 = (bf16[256,1024]{1,0:T(8,128)(2,1)S(1)}, bf16[256,1024]{1,0:T(8,128)(2,1)}, u32[]{:S(2)}, u32[]{:S(2)}) collective-permute-start(bf16[256,1024]{1,0:T(8,128)(2,1)S(1)} %constant_dynamic-update-slice_fusion.10.refs_0_), channel_id=1, source_target_pairs={{0,32},{1,33},{2,34},{3,35},{4,36},{5,37},{6,38},{7,39},{8,40},{9,... | collective-permute-start | bytes 1572872 | tf_op jit(solution)/shard_map/ppermute | solution.py:24
  114.5 15.3 %collective-permute-start.20 = (bf16[256,1024]{1,0:T(8,128)(2,1)S(1)}, bf16[256,1024]{1,0:T(8,128)(2,1)}, u32[]{:S(2)}, u32[]{:S(2)}) collective-permute-start(bf16[256,1024]{1,0:T(8,128)(2,1)S(1)} %collective-permute-done.16.refs_7_), channel_id=1, source_target_pairs={{0,1},{1,0},{2,3},{3,2},{4,5},{5,4},{6,7},{7,6},{8,9},{9,8},{10,11... | collective-permute-start | bytes 1572872 | tf_op jit(solution)/shard_map/ppermute | solution.py:24
  115.6 14.2 %collective-permute-start.19 = (bf16[256,1024]{1,0:T(8,128)(2,1)}, bf16[256,1024]{1,0:T(8,128)(2,1)}, u32[]{:S(2)}, u32[]{:S(2)}) collective-permute-start(bf16[256,1024]{1,0:T(8,128)(2,1)} %collective-permute-done.15.refs_6_), channel_id=1, source_target_pairs={{0,1},{1,0},{2,3},{3,2},{4,5},{5,4},{6,7},{7,6},{8,9},{9,8},{10,11... | collective-permute-start | bytes 1572872 | tf_op jit(solution)/shard_map/ppermute | solution.py:24
  115.6 14.2 %collective-permute-start.18 = (bf16[256,1024]{1,0:T(8,128)(2,1)}, bf16[256,1024]{1,0:T(8,128)(2,1)}, u32[]{:S(2)}, u32[]{:S(2)}) collective-permute-start(bf16[256,1024]{1,0:T(8,128)(2,1)} %collective-permute-done.14.refs_5_), channel_id=1, source_target_pairs={{0,1},{1,0},{2,3},{3,2},{4,5},{5,4},{6,7},{7,6},{8,9},{9,8},{10,11... | collective-permute-start | bytes 1572872 | tf_op jit(solution)/shard_map/ppermute | solution.py:24
  (17 other events, 192.2 us)
where the time goes:
time: 152 us; the launch traced here: 151 us
  starting transfers between devices  65.5 us (43%)
  waiting for transfers between devices  48.9 us (32%)
  Pallas kernels  21.5 us (14%)
  matrix products  10 us (7%)
  local copies, waits for them, and re-layouts  3.07 us (2%)
    ppermute x33, starting transfers between devices, move(): return lax.ppermute(value, ('row', 'col'), pairs)  65.5 us
    ppermute x33, waiting for transfers between devices, move(): return lax.ppermute(value, ('row', 'col'), pairs)  48.9 us
    pallas_call x1, Pallas kernels, finish(): pl.pallas_call(finish_kernel, grid_spec=pltpu.PrefetchScalarGridSpec(num_...  21.5 us
    dot_general x8, matrix products, mm(): return jnp.dot(a, b, preferred_element_type=F32)  9.45 us
  transfers between devices with their start and end apart: 33, of which 13 were waited for; matrix products, arithmetic and copies ran while one was open for 6% of the time, Pallas kernels for 0%

commit v1 on v0

--- a/solution.py
+++ b/solution.py
@@ -69,71 +69,128 @@
     return lambda x, zl, zh, y, k: (x, zl, zh ^ dz, y + step, k)
 
 
-def finish_kernel(spot, *refs):
-    pieces = refs[:12]
-    gram_ref, inverse_ref, sign_ref, trailing_ref, out_ref, panel_ref, strip_ref, now_ref = refs[12:]
-    t = pl.program_id(0)
-    for i in range(12):
-
-        @pl.when(t == i)
+def panel(cols, inverses, gram, sign):
+    first = mm(cols[:, :512], inverses[0]).astype(BF)
+    weighted = first * sign[:, :512]
+    coupled = (cols[:, 512:].astype(F32) - mm(weighted, gram[...])).astype(BF)
+    return first, mm(coupled, inverses[1]).astype(BF)
+
+
+def whole(value):
+    zeros = (0,) * value.ndim
+    return pl.BlockSpec(value.shape, lambda t, spot: zeros, pipeline_mode=pl.Buffered(1))
+
+
+def block_kernel(spot, *refs):
+    pieces = refs[:8]
+    gram, inverses, sign, out, now = refs[8:]
+    for half in range(2):
+
+        @pl.when(pl.program_id(0) == half)
         def _():
-            now_ref[...] = pieces[i][...]
-
-    sign = sign_ref[...]
-    first = mm(now_ref[:, :512], inverse_ref[0]).astype(BF)
-    first_signed = first * sign[:, :512]
-    coupled = (now_ref[:, 512:].astype(F32) - mm(first_signed, gram_ref[...])).astype(BF)
-    second = mm(coupled, inverse_ref[1]).astype(BF)
-
-    @pl.when(t < 4)
-    def _():
-        at = pl.ds(pl.multiple_of(spot[t] * 256, 256), 256)
-        strip_ref[at, :512] = first
-        strip_ref[at, 512:] = second
-
-    @pl.when(t >= 4)
-    def _():
-        panel_ref[:, :512] = first
-        panel_ref[:, 512:] = second
-        across = (((1,), (1,)), ((), ()))
-        update = lax.dot_general(
-            first_signed, strip_ref[:, :512], across, preferred_element_type=F32
-        )
-        update += lax.dot_general(
-            second * sign[:, 512:], strip_ref[:, 512:], across, preferred_element_type=F32
-        )
-        out_ref[...] = trailing_ref[...] + update
-
-
-def finish(spot, strips, block, gram_low, inverses, sign, trailing):
-    def whole(value):
-        zeros = (0,) * value.ndim
-        return pl.BlockSpec(
-            value.shape, lambda t, spot: zeros, pipeline_mode=pl.Buffered(1)
-        )
-
-    def tile(width):
-        return pl.BlockSpec((256, width), lambda t, spot: (spot[jnp.maximum(t, 4)], 0))
-
-    fixed = [*strips, *block, gram_low, inverses, sign]
+            for i in range(4):
+                at = pl.ds(pl.multiple_of(spot[half * 4 + i] % 4 * 256, 256), 256)
+                now[at, :] = pieces[half * 4 + i][...]
+
+    for at in (slice(0, 512), slice(512, 1024)):
+        first, second = panel(now.at[at], inverses, gram, sign[...])
+        out[at, :512] = first
+        out[at, 512:] = second
+
+
+def block_panels(spot, pieces, gram, inverses, sign):
+    fixed = [*pieces, gram, inverses, sign]
     return pl.pallas_call(
-        finish_kernel,
+        block_kernel,
         grid_spec=pltpu.PrefetchScalarGridSpec(
             num_scalar_prefetch=1,
-            grid=(12,),
-            in_specs=[whole(value) for value in fixed] + [tile(1024)],
-            out_specs=[tile(1024), tile(1024)],
-            scratch_shapes=[pltpu.VMEM((1024, 1024), BF), pltpu.VMEM((256, 1024), BF)],
-        ),
-        out_shape=(
-            jax.ShapeDtypeStruct((2048, 1024), F32),
-            jax.ShapeDtypeStruct((2048, 1024), BF),
-        ),
-        compiler_params=pltpu.CompilerParams(vmem_limit_bytes=40 * 2**20),
+            grid=(2,),
+            in_specs=[whole(value) for value in fixed],
+            out_specs=pl.BlockSpec((1024, 1024), lambda t, spot: (spot[4 * t] // 4, 0)),
+            scratch_shapes=[pltpu.VMEM((1024, 1024), BF)],
+        ),
+        out_shape=jax.ShapeDtypeStruct((2048, 1024), BF),
+        compiler_params=pltpu.CompilerParams(vmem_limit_bytes=32 * 2**20),
         cost_estimate=pl.CostEstimate(
-            flops=9_000_000_000, bytes_accessed=26 * 2**20, transcendentals=0
-        ),
-    )(spot, *fixed, trailing)
+            flops=3_200_000_000, bytes_accessed=9 * 2**20, transcendentals=0
+        ),
+    )(spot, *fixed)
+
+
+SLAB = 512
+SLABS = 2048 // SLAB
+
+
+def slab_kernel(spot, *refs):
+    strips = refs[:5]
+    gram, inverses, sign, panels, trailing, out = refs[5:11]
+    cols, strip, panel_here, slab, panel_sem, load_sem, save_sem = refs[11:]
+
+    def loads(i):
+        at = pl.ds(i * SLAB, SLAB)
+        return (
+            pltpu.make_async_copy(panels.at[at], panel_here.at[at], panel_sem.at[i]),
+            pltpu.make_async_copy(trailing.at[at], slab.at[at], load_sem.at[i]),
+        )
+
+    def save(i):
+        at = pl.ds(i * SLAB, SLAB)
+        return pltpu.make_async_copy(slab.at[at], out.at[at], save_sem.at[i])
+
+    for i in range(SLABS):
+        for copy in loads(i):
+            copy.start()
+    for i, piece in enumerate(strips):
+        height = piece.shape[0]
+        cols[pl.ds(pl.multiple_of(spot[i] * 128, 128), height), :] = piece[...]
+    first, second = panel(cols, inverses, gram, sign[...])
+    strip[:, :512] = first * sign[:, :512]
+    strip[:, 512:] = second * sign[:, 512:]
+
+    def step(i, carry):
+        for copy in loads(i):
+            copy.wait()
+        at = pl.ds(pl.multiple_of(i * SLAB, SLAB), SLAB)
+        slab[at, :] = slab[at, :] + lax.dot_general(
+            panel_here[at, :],
+            strip[...],
+            (((1,), (1,)), ((), ())),
+            preferred_element_type=F32,
+        )
+        save(i).start()
+        return carry
+
+    lax.fori_loop(0, SLABS, step, 0)
+    for i in range(SLABS):
+        save(i).wait()
+
+
+def update_slab(spot, strips, gram, inverses, sign, panels, trailing):
+    fixed = [*strips, gram, inverses, sign]
+    anywhere = pl.BlockSpec(memory_space=pl.ANY)
+    return pl.pallas_call(
+        slab_kernel,
+        grid_spec=pltpu.PrefetchScalarGridSpec(
+            num_scalar_prefetch=1,
+            grid=(1,),
+            in_specs=[whole(value) for value in fixed] + [anywhere] * 2,
+            out_specs=anywhere,
+            scratch_shapes=[
+                pltpu.VMEM((1024, 1024), BF),
+                pltpu.VMEM((1024, 1024), BF),
+                pltpu.VMEM((2048, 1024), BF),
+                pltpu.VMEM((2048, 1024), F32),
+                pltpu.SemaphoreType.DMA((SLABS,)),
+                pltpu.SemaphoreType.DMA((SLABS,)),
+                pltpu.SemaphoreType.DMA((SLABS,)),
+            ],
+        ),
+        out_shape=jax.ShapeDtypeStruct((2048, 1024), F32),
+        compiler_params=pltpu.CompilerParams(vmem_limit_bytes=58 * 2**20),
+        cost_estimate=pl.CostEstimate(
+            flops=6_000_000_000, bytes_accessed=24 * 2**20, transcendentals=0
+        ),
+    )(spot, *fixed, panels, trailing)
 
 
 def body(a_cols, owners, column_slot, update_flag, rescale, inverses, trailing):
@@ -169,7 +226,9 @@
     piece = move(cols, to_strip)
     strip = put(jnp.zeros((256, 1024), BF), piece, part * 128)
     strip = put(strip, move(piece, other_zl), (1 - part) * 128)
-    strips = [strip] + [move(strip, along_x(step)) for step in (1, 2, 3)]
+    strips = [strip] + [move(strip, along_x(step)) for step in (1, 3)]
+    across = move(piece, along_x(2))
+    strips += [across, move(across, other_zl)]
 
     near = [pair] + [move(pair, along_y(step)) for step in (1, 2, 3)]
     far = [move(value, other_core) for value in near]
@@ -194,14 +253,15 @@
     low4 = put(jnp.zeros((512, 512), BF), low3, k * 256)
     gram_low = put(low4, move(low3, other_core), (1 - k) * 256)
 
-    tile = lax.iota(jnp.int32, 12)
-    step = tile % 4
-    spot = jnp.where(
-        tile < 4,
-        (x - step - first) % 4,
-        jnp.where(tile < 8, k, 1 - k) * 4 + (y - step) % 4,
-    )
-    return finish(spot, strips, near + far, gram_low, inverses, signed[None, :], trailing)
+    index = lax.iota(jnp.int32, 8)
+    block_spot = jnp.where(index < 4, k, 1 - k) * 4 + (y - index) % 4
+    hop = jnp.where(index < 3, (index * index + index) // 2, 2)
+    lower = jnp.where(index == 3, part, jnp.where(index == 4, 1 - part, 0))
+    strip_spot = (x - hop - first) % 4 * 2 + lower
+    sign = signed[None, :]
+    panels = block_panels(block_spot, near + far, gram_low, inverses, sign)
+    slab = update_slab(strip_spot, strips, gram_low, inverses, sign, panels, trailing)
+    return slab, panels
 
 
 def solution(mesh):

time: 152 us -> 155 us (1.020)
  waiting for transfers between devices: 48.9 us -> 58.4 us
  starting transfers between devices: 65.5 us -> 57.4 us
  local copies, waits for them, and re-layouts: 3.07 us -> 7.44 us
  Pallas kernels: 21.5 us -> 18.6 us
    ppermute x33 -> x34, waiting for transfers between devices: 48.9 us -> 58.4 us  [move(): return lax.ppermute(value, ('row', 'col'), pairs)]
    ppermute x33 -> x34, starting transfers between devices: 65.5 us -> 57.4 us  [move(): return lax.ppermute(value, ('row', 'col'), pairs)]
    pallas_call x1 -> x2, Pallas kernels: 21.5 us -> 18.6 us  [the longest x1 11.2 us: update_slab(): pl.pallas_call(slab_kernel, grid_spec=pltpu.PrefetchScalarGridSpec(num_sc...]
    dynamic_update_slice x9, local copies, waits for them, and re-layouts: 1.11 us -> 3.01 us  [put(): return lax.dynamic_update_slice_in_dim(buffer, piece, start, 0)]
  transfers between devices with their start and end apart: 33 -> 34, of which waited for: 13 -> 15; matrix products, arithmetic and copies ran while one was open for 6% -> 8% of each run, Pallas kernels for 0% -> 5%
where the time goes in v1:
time: 155 us
  waiting for transfers between devices  58.4 us (38%)
  starting transfers between devices  57.4 us (37%)
  Pallas kernels  18.6 us (12%)
  matrix products  10 us (6%)
  local copies, waits for them, and re-layouts  7.44 us (5%)
  other arithmetic  1.71 us (1%)
    ppermute x34, waiting for transfers between devices, move(): return lax.ppermute(value, ('row', 'col'), pairs)  58.4 us
    ppermute x34, starting transfers between devices, move(): return lax.ppermute(value, ('row', 'col'), pairs)  57.4 us
    pallas_call x1, Pallas kernels, update_slab(): pl.pallas_call(slab_kernel, grid_spec=pltpu.PrefetchScalarGridSpec(num_sc...  11.2 us
    dot_general x8, matrix products, mm(): return jnp.dot(a, b, preferred_element_type=F32)  9.43 us
    pallas_call x1, Pallas kernels, block_panels(): pl.pallas_call(block_kernel, grid_spec=pltpu.PrefetchScalarGridSpec(num_s...  7.36 us
  transfers between devices with their start and end apart: 34, of which 15 were waited for; matrix products, arithmetic and copies ran while one was open for 8% of the time, Pallas kernels for 5%

profile of v1, /device:TPU:1, one launch (start us, length us, event | category | flops | bytes accessed | tf_op | source)
XLA Modules:
  0.0 155.0 jit_solution(1887491312236996687)
XLA Ops:
  0.7 2.7 %constant_dynamic-slice_fusion.4 = (bf16[1024,512]{1,0:T(8,128)(2,1)}, bf16[1024,512]{1,0:T(8,128)(2,1)S(1)}) fusion(bf16[2048,512]{1,0:T(8,128)(2,1)} %param.7, s32[]{:T(128)S(6)} %select_n.261, s32[]{:T(128)S(6)} %select_n.260), kind=kLoop, calls=%fused_computation.84 | loop fusion | bytes 4194312 | tf_op jit(solution)/shard_map/dynamic_slice | solution.py:57
  4.8 2.4 %collective-permute-done = bf16[1024,512]{1,0:T(8,128)(2,1)S(1)} collective-permute-done((bf16[1024,512]{1,0:T(8,128)(2,1)}, bf16[1024,512]{1,0:T(8,128)(2,1)S(1)}, u32[]{:S(2)}, u32[]{:S(2)}) %collective-permute-start) | collective-permute-done | bytes 1048608 | tf_op jit(solution)/shard_map/ppermute | solution.py:24
  7.2 6.2 %collective-permute-start.7 = (bf16[128,1024]{1,0:T(8,128)(2,1)S(1)}, bf16[128,1024]{1,0:T(8,128)(2,1)}, u32[]{:S(2)}, u32[]{:S(2)}) collective-permute-start(bf16[128,1024]{1,0:T(8,128)(2,1)S(1)} %fusion.30), channel_id=1, source_target_pairs={{0,14},{1,15},{2,8},{3,9},{4,10},{5,11},{6,12},{7,13},{8,6},{9,7},... | collective-permute-start | bytes 786440 | tf_op jit(solution)/shard_map/ppermute | solution.py:24
  17.2 5.9 %collective-permute-done.7 = bf16[128,1024]{1,0:T(8,128)(2,1)} collective-permute-done((bf16[128,1024]{1,0:T(8,128)(2,1)S(1)}, bf16[128,1024]{1,0:T(8,128)(2,1)}, u32[]{:S(2)}, u32[]{:S(2)}) %collective-permute-start.7) | collective-permute-done | bytes 262176 | tf_op jit(solution)/shard_map/ppermute | solution.py:24
  23.1 1.9 %fusion.7 = f32[128,1024]{1,0:T(8,128)S(1)} fusion(bf16[128,1024]{1,0:T(8,128)(2,1)} %collective-permute-done.7, s32[1024]{0:T(1024)S(1)} %get-tuple-element.34), kind=kOutput, calls=%fused_computation.15 | convolution fusion | flops 269484032 | bytes 790528 | tf_op jit(solution)/shard_map/dot_general | solution.py:65
  25.0 2.5 %collective-permute-start.6 = (bf16[128,1024]{1,0:T(8,128)(2,1)S(1)}, bf16[128,1024]{1,0:T(8,128)(2,1)S(1)}, u32[]{:S(2)}, u32[]{:S(2)}) collective-permute-start(bf16[128,1024]{1,0:T(8,128)(2,1)S(1)} %get-tuple-element.22), channel_id=1, source_target_pairs={{0,12},{1,13},{2,14},{3,15},{4,8},{5,9},{6,10},{7,11},{8,4},{9,5},... | collective-permute-start | bytes 786440 | tf_op jit(solution)/shard_map/ppermute | solution.py:24
  27.4 1.9 %fusion.1 = f32[128,1024]{1,0:T(8,128)S(1)} fusion(bf16[128,1024]{1,0:T(8,128)(2,1)} %collective-permute-done.1, s32[1024]{0:T(1024)S(1)} %get-tuple-element.9), kind=kOutput, calls=%fused_computation.9 | convolution fusion | flops 269484032 | bytes 790528 | tf_op jit(solution)/shard_map/dot_general | solution.py:65
  32.2 6.0 %collective-permute-done.5 = bf16[128,1024]{1,0:T(8,128)(2,1)S(1)} collective-permute-done((bf16[128,1024]{1,0:T(8,128)(2,1)S(1)}, bf16[128,1024]{1,0:T(8,128)(2,1)S(1)}, u32[]{:S(2)}, u32[]{:S(2)}) %collective-permute-start.5) | collective-permute-done | bytes 262176 | tf_op jit(solution)/shard_map/ppermute | solution.py:24
  41.2 3.4 %collective-permute-start.14 = (bf16[128,1024]{1,0:T(8,128)(2,1)S(1)}, bf16[128,1024]{1,0:T(8,128)(2,1)S(1)}, u32[]{:S(2)}, u32[]{:S(2)}) collective-permute-start(bf16[128,1024]{1,0:T(8,128)(2,1)S(1)} %get-tuple-element.38), channel_id=1, source_target_pairs={{0,8},{1,9},{2,10},{3,11},{4,12},{5,13},{6,14},{7,15},{8,0},{9,1},... | collective-permute-start | bytes 786440 | tf_op jit(solution)/shard_map/ppermute | solution.py:24
  44.6 3.8 %collective-permute-done.14 = bf16[128,1024]{1,0:T(8,128)(2,1)S(1)} collective-permute-done((bf16[128,1024]{1,0:T(8,128)(2,1)S(1)}, bf16[128,1024]{1,0:T(8,128)(2,1)S(1)}, u32[]{:S(2)}, u32[]{:S(2)}) %collective-permute-start.14) | collective-permute-done | bytes 262176 | tf_op jit(solution)/shard_map/ppermute | solution.py:24
  49.1 5.5 %collective-permute-start.15 = (f32[256,256]{1,0:T(8,128)S(1)}, f32[256,256]{1,0:T(8,128)S(1)}, u32[]{:S(2)}, u32[]{:S(2)}) collective-permute-start(f32[256,256]{1,0:T(8,128)S(1)} %constant_dynamic-slice_fusion.3), channel_id=1, source_target_pairs={{0,1},{1,0},{2,3},{3,2},{4,5},{5,4},{6,7},{7,6},{8,9},{9,8},{10,11... | collective-permute-start | bytes 786440 | tf_op jit(solution)/shard_map/ppermute | solution.py:24
  55.9 2.7 %collective-permute-start.18 = (f32[64,256]{1,0:T(8,128)S(1)}, f32[64,256]{1,0:T(8,128)S(1)}, u32[]{:S(2)}, u32[]{:S(2)}) collective-permute-start(f32[64,256]{1,0:T(8,128)S(1)} %get-tuple-element.26), channel_id=1, source_target_pairs={{0,6},{1,7},{2,0},{3,1},{4,2},{5,3},{6,4},{7,5},{8,14},{9,15},{10,... | collective-permute-start | bytes 196616 | tf_op jit(solution)/shard_map/ppermute | solution.py:24
  60.2 3.0 %collective-permute-done.17 = f32[64,256]{1,0:T(8,128)S(1)} collective-permute-done((f32[64,256]{1,0:T(8,128)S(1)}, f32[64,256]{1,0:T(8,128)S(1)}, u32[]{:S(2)}, u32[]{:S(2)}) %collective-permute-start.17) | collective-permute-done | bytes 65568 | tf_op jit(solution)/shard_map/ppermute | solution.py:24
  69.6 6.0 %collective-permute-start.21 = (f32[64,256]{1,0:T(8,128)S(1)}, f32[64,256]{1,0:T(8,128)S(1)}, u32[]{:S(2)}, u32[]{:S(2)}) collective-permute-start(f32[64,256]{1,0:T(8,128)S(1)} %add.331), channel_id=1, source_target_pairs={{0,64},{1,65},{2,66},{3,67},{4,68},{5,69},{6,70},{7,71},{8,72},{9,... | collective-permute-start | bytes 196616 | tf_op jit(solution)/shard_map/ppermute | solution.py:24
  75.6 5.7 %collective-permute-start.12 = (bf16[128,1024]{1,0:T(8,128)(2,1)}, bf16[128,1024]{1,0:T(8,128)(2,1)S(1)}, u32[]{:S(2)}, u32[]{:S(2)}) collective-permute-start(bf16[128,1024]{1,0:T(8,128)(2,1)} %collective-permute-done.8), channel_id=1, source_target_pairs={{0,64},{1,65},{2,66},{3,67},{4,68},{5,69},{6,70},{7,71},{8,72},{9,... | collective-permute-start | bytes 786440 | tf_op jit(solution)/shard_map/ppermute | solution.py:24
  82.3 7.7 %collective-permute-start.29 = (bf16[256,1024]{1,0:T(8,128)(2,1)S(1)}, bf16[256,1024]{1,0:T(8,128)(2,1)S(1)}, u32[]{:S(2)}, u32[]{:S(2)}) collective-permute-start(bf16[256,1024]{1,0:T(8,128)(2,1)S(1)} %constant_dynamic-update-slice_fusion.8.refs_0_), channel_id=1, source_target_pairs={{0,6},{1,7},{2,0},{3,1},{4,2},{5,3},{6,4},{7,5},{8,14},{9,15},{10,... | collective-permute-start | bytes 1572872 | tf_op jit(solution)/shard_map/ppermute | solution.py:24
  90.7 2.1 %collective-permute-start.25 = (bf16[64,512]{1,0:T(8,128)(2,1)S(1)}, bf16[64,512]{1,0:T(8,128)(2,1)S(1)}, u32[]{:S(2)}, u32[]{:S(2)}) collective-permute-start(bf16[64,512]{1,0:T(8,128)(2,1)S(1)} %constant_dynamic-update-slice_fusion.6), channel_id=1, source_target_pairs={{0,6},{1,7},{2,0},{3,1},{4,2},{5,3},{6,4},{7,5},{8,14},{9,15},{10,... | collective-permute-start | bytes 196616 | tf_op jit(solution)/shard_map/ppermute | solution.py:24
  93.5 17.5 %collective-permute-done.25 = bf16[64,512]{1,0:T(8,128)(2,1)S(1)} collective-permute-done((bf16[64,512]{1,0:T(8,128)(2,1)S(1)}, bf16[64,512]{1,0:T(8,128)(2,1)S(1)}, u32[]{:S(2)}, u32[]{:S(2)}) %collective-permute-start.25) | collective-permute-done | bytes 65568 | tf_op jit(solution)/shard_map/ppermute | solution.py:24
  111.0 5.7 %collective-permute-done.23 = bf16[64,512]{1,0:T(8,128)(2,1)S(1)} collective-permute-done((bf16[64,512]{1,0:T(8,128)(2,1)S(1)}, bf16[64,512]{1,0:T(8,128)(2,1)S(1)}, u32[]{:S(2)}, u32[]{:S(2)}) %collective-permute-start.23) | collective-permute-done | bytes 65568 | tf_op jit(solution)/shard_map/ppermute | solution.py:24
  116.8 4.6 %collective-permute-done.24 = bf16[64,512]{1,0:T(8,128)(2,1)S(1)} collective-permute-done((bf16[64,512]{1,0:T(8,128)(2,1)S(1)}, bf16[64,512]{1,0:T(8,128)(2,1)S(1)}, u32[]{:S(2)}, u32[]{:S(2)}) %collective-permute-start.24) | collective-permute-done | bytes 65568 | tf_op jit(solution)/shard_map/ppermute | solution.py:24
  121.4 2.6 %collective-permute-start.30 = (bf16[256,1024]{1,0:T(8,128)(2,1)S(1)}, bf16[256,1024]{1,0:T(8,128)(2,1)}, u32[]{:S(2)}, u32[]{:S(2)}) collective-permute-start(bf16[256,1024]{1,0:T(8,128)(2,1)S(1)} %constant_dynamic-update-slice_fusion.8.refs_0_), channel_id=1, source_target_pairs={{0,1},{1,0},{2,3},{3,2},{4,5},{5,4},{6,7},{7,6},{8,9},{9,8},{10,11... | collective-permute-start | bytes 1572872 | tf_op jit(solution)/shard_map/ppermute | solution.py:24
  130.4 7.4 %shard_map.86.refs_8_ = bf16[2048,1024]{1,0:T(8,128)(2,1)} custom-call(s32[8]{0:T(128)S(1)} %fusion.53.spot, bf16[256,1024]{1,0:T(8,128)(2,1)S(1)} %constant_dynamic-update-slice_fusion.8.refs_0_, bf16[256,1024]{1,0:T(8,128)(2,1)S(1)} %collective-permute-done.27.refs_1_, bf16[256,1024]{1,0:T(8,128)(2,1)S(1)} %collective-permute-done.28.refs_2_, ...), custom_call_target="tpu_custom_call" | custom-call | flops 3200000000 | bytes 9437184 | tf_op jit(solution)/shard_map/pallas_call | solution.py:103
  137.8 3.3 %collective-permute-done.11.refs_2_ = bf16[256,1024]{1,0:T(8,128)(2,1)S(1)} collective-permute-done((bf16[256,1024]{1,0:T(8,128)(2,1)S(1)}, bf16[256,1024]{1,0:T(8,128)(2,1)S(1)}, u32[]{:S(2)}, u32[]{:S(2)}) %collective-permute-start.11) | collective-permute-done | bytes 524320 | tf_op jit(solution)/shard_map/ppermute | solution.py:24
  143.6 11.2 %shard_map.87 = f32[2048,1024]{1,0:T(8,128)} custom-call(s32[8]{0:T(128)} %fusion.58.spot, bf16[256,1024]{1,0:T(8,128)(2,1)} %copy-done.5, bf16[256,1024]{1,0:T(8,128)(2,1)} %copy-done.7, bf16[256,1024]{1,0:T(8,128)(2,1)} %copy-done.6, bf16[128,1024]{1,0:T(8,128)(2,1)} %copy-done.8, bf16[128,1024]{1,0:T(8,128)(2,1)} %copy-done.9, bf16[512,512]{1,0:T(8,128)(2,1)} %copy-done, ...), custom_call_target="tpu_custom_call" | custom-call | flops 6000000000 | bytes 25165824 | tf_op jit(solution)/shard_map/pallas_call | solution.py:171
  (115 shorter events, 32.1 us)
Async XLA Ops:
  7.2 15.8 %collective-permute-start.7 = (bf16[128,1024]{1,0:T(8,128)(2,1)S(1)}, bf16[128,1024]{1,0:T(8,128)(2,1)}, u32[]{:S(2)}, u32[]{:S(2)}) collective-permute-start(bf16[128,1024]{1,0:T(8,128)(2,1)S(1)} %fusion.30), channel_id=1, source_target_pairs={{0,14},{1,15},{2,8},{3,9},{4,10},{5,11},{6,12},{7,13},{8,6},{9,7},... | collective-permute-start | bytes 786440 | tf_op jit(solution)/shard_map/ppermute | solution.py:24
  14.5 10.5 %collective-permute-start.1 = (bf16[128,1024]{1,0:T(8,128)(2,1)}, bf16[128,1024]{1,0:T(8,128)(2,1)}, u32[]{:S(2)}, u32[]{:S(2)}) collective-permute-start(bf16[128,1024]{1,0:T(8,128)(2,1)} %get-tuple-element.17), channel_id=1, source_target_pairs={{0,2},{1,3},{2,4},{3,5},{4,6},{5,7},{6,0},{7,1},{8,10},{9,11},{10,... | collective-permute-start | bytes 786440 | tf_op jit(solution)/shard_map/ppermute | solution.py:24
  14.5 14.8 %collective-permute-start.2 = (bf16[128,1024]{1,0:T(8,128)(2,1)}, bf16[128,1024]{1,0:T(8,128)(2,1)S(1)}, u32[]{:S(2)}, u32[]{:S(2)}) collective-permute-start(bf16[128,1024]{1,0:T(8,128)(2,1)} %get-tuple-element.18), channel_id=1, source_target_pairs={{0,4},{1,5},{2,6},{3,7},{4,0},{5,1},{6,2},{7,3},{8,12},{9,13},{10,... | collective-permute-start | bytes 786440 | tf_op jit(solution)/shard_map/ppermute | solution.py:24
  16.1 14.1 %collective-permute-start.3 = (bf16[128,1024]{1,0:T(8,128)(2,1)S(1)}, bf16[128,1024]{1,0:T(8,128)(2,1)S(1)}, u32[]{:S(2)}, u32[]{:S(2)}) collective-permute-start(bf16[128,1024]{1,0:T(8,128)(2,1)S(1)} %get-tuple-element.19), channel_id=1, source_target_pairs={{0,6},{1,7},{2,0},{3,1},{4,2},{5,3},{6,4},{7,5},{8,14},{9,15},{10,... | collective-permute-start | bytes 786440 | tf_op jit(solution)/shard_map/ppermute | solution.py:24
  17.2 14.0 %collective-permute-start.4 = (bf16[128,1024]{1,0:T(8,128)(2,1)S(1)}, bf16[128,1024]{1,0:T(8,128)(2,1)S(1)}, u32[]{:S(2)}, u32[]{:S(2)}) collective-permute-start(bf16[128,1024]{1,0:T(8,128)(2,1)S(1)} %get-tuple-element.20), channel_id=1, source_target_pairs={{0,8},{1,9},{2,10},{3,11},{4,12},{5,13},{6,14},{7,15},{8,0},{9,1},... | collective-permute-start | bytes 786440 | tf_op jit(solution)/shard_map/ppermute | solution.py:24
  23.1 15.1 %collective-permute-start.5 = (bf16[128,1024]{1,0:T(8,128)(2,1)S(1)}, bf16[128,1024]{1,0:T(8,128)(2,1)S(1)}, u32[]{:S(2)}, u32[]{:S(2)}) collective-permute-start(bf16[128,1024]{1,0:T(8,128)(2,1)S(1)} %get-tuple-element.21), channel_id=1, source_target_pairs={{0,10},{1,11},{2,12},{3,13},{4,14},{5,15},{6,8},{7,9},{8,2},{9,3},... | collective-permute-start | bytes 786440 | tf_op jit(solution)/shard_map/ppermute | solution.py:24
  25.0 14.1 %collective-permute-start.6 = (bf16[128,1024]{1,0:T(8,128)(2,1)S(1)}, bf16[128,1024]{1,0:T(8,128)(2,1)S(1)}, u32[]{:S(2)}, u32[]{:S(2)}) collective-permute-start(bf16[128,1024]{1,0:T(8,128)(2,1)S(1)} %get-tuple-element.22), channel_id=1, source_target_pairs={{0,12},{1,13},{2,14},{3,15},{4,8},{5,9},{6,10},{7,11},{8,4},{9,5},... | collective-permute-start | bytes 786440 | tf_op jit(solution)/shard_map/ppermute | solution.py:24
  41.2 7.2 %collective-permute-start.14 = (bf16[128,1024]{1,0:T(8,128)(2,1)S(1)}, bf16[128,1024]{1,0:T(8,128)(2,1)S(1)}, u32[]{:S(2)}, u32[]{:S(2)}) collective-permute-start(bf16[128,1024]{1,0:T(8,128)(2,1)S(1)} %get-tuple-element.38), channel_id=1, source_target_pairs={{0,8},{1,9},{2,10},{3,11},{4,12},{5,13},{6,14},{7,15},{8,0},{9,1},... | collective-permute-start | bytes 786440 | tf_op jit(solution)/shard_map/ppermute | solution.py:24
  49.1 6.7 %collective-permute-start.15 = (f32[256,256]{1,0:T(8,128)S(1)}, f32[256,256]{1,0:T(8,128)S(1)}, u32[]{:S(2)}, u32[]{:S(2)}) collective-permute-start(f32[256,256]{1,0:T(8,128)S(1)} %constant_dynamic-slice_fusion.3), channel_id=1, source_target_pairs={{0,1},{1,0},{2,3},{3,2},{4,5},{5,4},{6,7},{7,6},{8,9},{9,8},{10,11... | collective-permute-start | bytes 786440 | tf_op jit(solution)/shard_map/ppermute | solution.py:24
  67.7 7.9 %collective-permute-start.8 = (bf16[128,1024]{1,0:T(8,128)(2,1)S(1)}, bf16[128,1024]{1,0:T(8,128)(2,1)}, u32[]{:S(2)}, u32[]{:S(2)}) collective-permute-start(bf16[128,1024]{1,0:T(8,128)(2,1)S(1)} %get-tuple-element.38), channel_id=1, source_target_pairs={{0,0},{1,1},{2,32},{3,33},{4,64},{5,65},{6,96},{7,97},{8,16},{9,17... | collective-permute-start | bytes 786440 | tf_op jit(solution)/shard_map/ppermute | solution.py:24
  69.6 11.6 %collective-permute-start.21 = (f32[64,256]{1,0:T(8,128)S(1)}, f32[64,256]{1,0:T(8,128)S(1)}, u32[]{:S(2)}, u32[]{:S(2)}) collective-permute-start(f32[64,256]{1,0:T(8,128)S(1)} %add.331), channel_id=1, source_target_pairs={{0,64},{1,65},{2,66},{3,67},{4,68},{5,69},{6,70},{7,71},{8,72},{9,... | collective-permute-start | bytes 196616 | tf_op jit(solution)/shard_map/ppermute | solution.py:24
  75.6 17.2 %collective-permute-start.12 = (bf16[128,1024]{1,0:T(8,128)(2,1)}, bf16[128,1024]{1,0:T(8,128)(2,1)S(1)}, u32[]{:S(2)}, u32[]{:S(2)}) collective-permute-start(bf16[128,1024]{1,0:T(8,128)(2,1)} %collective-permute-done.8), channel_id=1, source_target_pairs={{0,64},{1,65},{2,66},{3,67},{4,68},{5,69},{6,70},{7,71},{8,72},{9,... | collective-permute-start | bytes 786440 | tf_op jit(solution)/shard_map/ppermute | solution.py:24
  81.3 9.4 %collective-permute-start.22 = (bf16[64,256]{1,0:T(8,128)(2,1)S(1)}, bf16[64,256]{1,0:T(8,128)(2,1)S(1)}, u32[]{:S(2)}, u32[]{:S(2)}) collective-permute-start(bf16[64,256]{1,0:T(8,128)(2,1)S(1)} %get-tuple-element.3), channel_id=1, source_target_pairs={{0,8},{1,9},{2,10},{3,11},{4,12},{5,13},{6,14},{7,15},{8,0},{9,1},... | collective-permute-start | bytes 98312 | tf_op jit(solution)/shard_map/ppermute | solution.py:24
  82.3 41.7 %collective-permute-start.29 = (bf16[256,1024]{1,0:T(8,128)(2,1)S(1)}, bf16[256,1024]{1,0:T(8,128)(2,1)S(1)}, u32[]{:S(2)}, u32[]{:S(2)}) collective-permute-start(bf16[256,1024]{1,0:T(8,128)(2,1)S(1)} %constant_dynamic-update-slice_fusion.8.refs_0_), channel_id=1, source_target_pairs={{0,6},{1,7},{2,0},{3,1},{4,2},{5,3},{6,4},{7,5},{8,14},{9,15},{10,... | collective-permute-start | bytes 1572872 | tf_op jit(solution)/shard_map/ppermute | solution.py:24
  90.0 34.1 %collective-permute-start.28 = (bf16[256,1024]{1,0:T(8,128)(2,1)S(1)}, bf16[256,1024]{1,0:T(8,128)(2,1)S(1)}, u32[]{:S(2)}, u32[]{:S(2)}) collective-permute-start(bf16[256,1024]{1,0:T(8,128)(2,1)S(1)} %constant_dynamic-update-slice_fusion.8.refs_0_), channel_id=1, source_target_pairs={{0,4},{1,5},{2,6},{3,7},{4,0},{5,1},{6,2},{7,3},{8,12},{9,13},{10,... | collective-permute-start | bytes 1572872 | tf_op jit(solution)/shard_map/ppermute | solution.py:24
  90.0 34.6 %collective-permute-start.27 = (bf16[256,1024]{1,0:T(8,128)(2,1)S(1)}, bf16[256,1024]{1,0:T(8,128)(2,1)S(1)}, u32[]{:S(2)}, u32[]{:S(2)}) collective-permute-start(bf16[256,1024]{1,0:T(8,128)(2,1)S(1)} %constant_dynamic-update-slice_fusion.8.refs_0_), channel_id=1, source_target_pairs={{0,2},{1,3},{2,4},{3,5},{4,6},{5,7},{6,0},{7,1},{8,10},{9,11},{10,... | collective-permute-start | bytes 1572872 | tf_op jit(solution)/shard_map/ppermute | solution.py:24
  90.7 20.3 %collective-permute-start.25 = (bf16[64,512]{1,0:T(8,128)(2,1)S(1)}, bf16[64,512]{1,0:T(8,128)(2,1)S(1)}, u32[]{:S(2)}, u32[]{:S(2)}) collective-permute-start(bf16[64,512]{1,0:T(8,128)(2,1)S(1)} %constant_dynamic-update-slice_fusion.6), channel_id=1, source_target_pairs={{0,6},{1,7},{2,0},{3,1},{4,2},{5,3},{6,4},{7,5},{8,14},{9,15},{10,... | collective-permute-start | bytes 196616 | tf_op jit(solution)/shard_map/ppermute | solution.py:24
  93.5 23.3 %collective-permute-start.23 = (bf16[64,512]{1,0:T(8,128)(2,1)S(1)}, bf16[64,512]{1,0:T(8,128)(2,1)S(1)}, u32[]{:S(2)}, u32[]{:S(2)}) collective-permute-start(bf16[64,512]{1,0:T(8,128)(2,1)S(1)} %constant_dynamic-update-slice_fusion.6), channel_id=1, source_target_pairs={{0,2},{1,3},{2,4},{3,5},{4,6},{5,7},{6,0},{7,1},{8,10},{9,11},{10,... | collective-permute-start | bytes 196616 | tf_op jit(solution)/shard_map/ppermute | solution.py:24
  111.0 13.7 %collective-permute-start.9 = (bf16[128,1024]{1,0:T(8,128)(2,1)}, bf16[128,1024]{1,0:T(8,128)(2,1)}, u32[]{:S(2)}, u32[]{:S(2)}) collective-permute-start(bf16[128,1024]{1,0:T(8,128)(2,1)} %collective-permute-done.8), channel_id=1, source_target_pairs={{0,16},{1,17},{2,18},{3,19},{4,20},{5,21},{6,22},{7,23},{8,24},{9,... | collective-permute-start | bytes 786440 | tf_op jit(solution)/shard_map/ppermute | solution.py:24
  121.4 6.3 %collective-permute-start.30 = (bf16[256,1024]{1,0:T(8,128)(2,1)S(1)}, bf16[256,1024]{1,0:T(8,128)(2,1)}, u32[]{:S(2)}, u32[]{:S(2)}) collective-permute-start(bf16[256,1024]{1,0:T(8,128)(2,1)S(1)} %constant_dynamic-update-slice_fusion.8.refs_0_), channel_id=1, source_target_pairs={{0,1},{1,0},{2,3},{3,2},{4,5},{5,4},{6,7},{7,6},{8,9},{9,8},{10,11... | collective-permute-start | bytes 1572872 | tf_op jit(solution)/shard_map/ppermute | solution.py:24
  124.0 6.3 %collective-permute-start.33 = (bf16[256,1024]{1,0:T(8,128)(2,1)S(1)}, bf16[256,1024]{1,0:T(8,128)(2,1)}, u32[]{:S(2)}, u32[]{:S(2)}) collective-permute-start(bf16[256,1024]{1,0:T(8,128)(2,1)S(1)} %collective-permute-done.29.refs_3_), channel_id=1, source_target_pairs={{0,1},{1,0},{2,3},{3,2},{4,5},{5,4},{6,7},{7,6},{8,9},{9,8},{10,11... | collective-permute-start | bytes 1572872 | tf_op jit(solution)/shard_map/ppermute | solution.py:24
  127.7 13.4 %collective-permute-start.11 = (bf16[256,1024]{1,0:T(8,128)(2,1)S(1)}, bf16[256,1024]{1,0:T(8,128)(2,1)S(1)}, u32[]{:S(2)}, u32[]{:S(2)}) collective-permute-start(bf16[256,1024]{1,0:T(8,128)(2,1)S(1)} %constant_dynamic-update-slice_fusion.10.refs_0_), channel_id=1, source_target_pairs={{0,96},{1,97},{2,98},{3,99},{4,100},{5,101},{6,102},{7,103},{8,104... | collective-permute-start | bytes 1572872 | tf_op jit(solution)/shard_map/ppermute | solution.py:24
  128.3 14.5 %collective-permute-start.10 = (bf16[256,1024]{1,0:T(8,128)(2,1)S(1)}, bf16[256,1024]{1,0:T(8,128)(2,1)S(1)}, u32[]{:S(2)}, u32[]{:S(2)}) collective-permute-start(bf16[256,1024]{1,0:T(8,128)(2,1)S(1)} %constant_dynamic-update-slice_fusion.10.refs_0_), channel_id=1, source_target_pairs={{0,32},{1,33},{2,34},{3,35},{4,36},{5,37},{6,38},{7,39},{8,40},{9,... | collective-permute-start | bytes 1572872 | tf_op jit(solution)/shard_map/ppermute | solution.py:24
  130.3 7.5 %collective-permute-start.13 = (bf16[128,1024]{1,0:T(8,128)(2,1)}, bf16[128,1024]{1,0:T(8,128)(2,1)S(1)}, u32[]{:S(2)}, u32[]{:S(2)}) collective-permute-start(bf16[128,1024]{1,0:T(8,128)(2,1)} %copy-done.8), channel_id=1, source_target_pairs={{0,16},{1,17},{2,18},{3,19},{4,20},{5,21},{6,22},{7,23},{8,24},{9,... | collective-permute-start | bytes 786440 | tf_op jit(solution)/shard_map/ppermute | solution.py:24
  (24 other events, 175.5 us)
